TPU v7x, 256 devices: a whole 4x4x8 slice. The times are simulated.
256 devices in a mesh: chan: 128 (over z, y, x_lo, core), stn: 2 (over x_hi).
Axes of the slice: x: 4 (x_hi: 2, x_lo: 2; x = x_hi * 2 + x_lo), y: 4, z: 8, core: 2. Of those that a mesh axis runs over, the one named last changes fastest.
Arguments:
- voltages: bfloat16 [2, 1536, 2, 256, 512], P(None, 'chan', None, None, 'stn'), may hold values from -6 to 6
- delay_table: float32 [4096], replicated, may hold values from -8 to 8
- delay_index: int32 [64, 512], P(None, 'stn'), may hold values from 0 to 4094
- delay_fraction: int32 [64, 512], P(None, 'stn'), may hold values from 0 to 65535
- station_subarray: int32 [512], P('stn'), may hold values from 0 to 3
Outputs:
- beams: bfloat16 [2, 64, 2, 256, 1536], P(None, 'stn', None, 'chan')
All inputs are finite; a program needn't handle non-finite values.
Results may differ from a plain program's by a relative error of at most 0.0068.
Values may be sent and summed in bfloat16 or wider, within the bound.
A program may use at most 128 MiB of HBM per device.

v0:
```python
import math
import jax
import jax.numpy as jnp
from jax import lax
from jax.sharding import Mesh
from jax.sharding import PartitionSpec as P

STATIONS = 512
POL = 2
NFFT = 256
TAPS = 12
GROUPS = 4
CHAN = ("chan_0", "chan_1", "chan_2", "chan_3")


def joined_along(parts, dim):
    shape = list(parts.shape[1:])
    shape[dim] *= parts.shape[0]
    return jnp.moveaxis(parts, 0, dim).reshape(shape)


def all_blocks(x, axes, turns):
    parts = x[None]
    for k in turns:
        parts = lax.all_gather(parts, axes[k], axis=0, tiled=True)
    held = [lax.axis_size(axes[k]) for k in reversed(turns)]
    parts = parts.reshape(*held, *x.shape)
    turned = sorted(range(len(turns)), key=lambda place: turns[len(turns) - 1 - place])
    return parts.transpose(*turned, *range(len(turns), parts.ndim)).reshape(-1, *x.shape)


def gather_axes(x, axes, turns, dim):
    return joined_along(all_blocks(x, axes, turns), dim)


def passed_along(value, axis, steps):
    count = lax.axis_size(axis)
    initial, last = (max(0, -steps), min(count, count - steps))
    return lax.ppermute(value, axis, [(source, source + steps) for source in range(initial, last)])


def in_blocks(x, dim, peers):
    shape = x.shape
    parts = x.reshape(*shape[:dim], peers, shape[dim] // peers, *shape[dim + 1 :])
    return jnp.moveaxis(parts, dim, 0)


def sent_and_summed(x, axis, dim):
    parts = in_blocks(x, dim, lax.axis_size(axis))
    arrived = lax.all_to_all(parts, axis, split_axis=0, concat_axis=0, tiled=True)
    return arrived.sum(axis=0)


def prototype(tap_count, points):
    length = tap_count * points
    sample_ids = jnp.arange(length, dtype=jnp.float32)
    centred = (sample_ids - (length - 1) / 2.0) / points
    window = 0.5 - 0.5 * jnp.cos(2.0 * math.pi * (sample_ids + 0.5) / length)
    coeffs = jnp.sinc(centred) * window
    coeffs = coeffs * jnp.sqrt(points / jnp.sum(coeffs * coeffs))
    return coeffs.reshape(tap_count, points)


def dft_table(points):
    indices = jnp.arange(points, dtype=jnp.int32)
    product = indices[:, None] * indices[None, :] % points
    angles = 2.0 * math.pi / points * product.astype(jnp.float32)
    cosine = jnp.cos(angles) / math.sqrt(points)
    sine_part = jnp.sin(angles) / math.sqrt(points)
    real_input = jnp.stack([cosine, -sine_part], axis=1)
    imag_input = jnp.stack([sine_part, cosine], axis=1)
    return jnp.stack([real_input, imag_input], axis=0).astype(jnp.bfloat16)


def polyphase(padded, coeffs, frame_count):
    summed = jnp.zeros(padded.shape[:1] + (frame_count,) + padded.shape[2:], jnp.float32)
    for tap_index in range(coeffs.shape[0]):
        summed = summed + coeffs[tap_index][:, None] * padded[
            :, tap_index : tap_index + frame_count
        ].astype(jnp.float32)
    return summed.astype(jnp.bfloat16)


def steering(delays, station_subarray, channel_ids):
    beam_ids = jnp.arange(delays.shape[0], dtype=jnp.int32)
    member = (station_subarray[None, :] == (beam_ids % GROUPS)[:, None]).astype(
        jnp.float32
    ) * math.sqrt(GROUPS / STATIONS)
    signed = (channel_ids + NFFT // 2) % NFFT - NFFT // 2
    frequency = signed.astype(jnp.float32) / NFFT
    phases = -2.0 * math.pi * frequency[:, None, None] * delays[None, :, :]
    real_weight = (member * jnp.cos(phases)).astype(jnp.bfloat16)
    imag_weight = (member * jnp.sin(phases)).astype(jnp.bfloat16)
    first_row = jnp.stack([real_weight, -imag_weight], axis=2)
    second_row = jnp.stack([imag_weight, real_weight], axis=2)
    return jnp.stack([first_row, second_row], axis=1)


def shards(voltages, delay_table, delay_index, delay_fraction, station_subarray):
    frames_dev = voltages.shape[1]
    local_stations = voltages.shape[4]
    beam_count = delay_index.shape[0]
    groups_chan = lax.axis_size(CHAN)
    per_dev = NFFT // groups_chan
    share = beam_count * local_stations // groups_chan
    first_entry = lax.axis_index(CHAN) * share
    index_share = lax.dynamic_slice_in_dim(delay_index.reshape(-1), first_entry, share, 0)
    fraction_share = lax.dynamic_slice_in_dim(delay_fraction.reshape(-1), first_entry, share, 0)
    lower_delay = jnp.take(delay_table, index_share, axis=0)
    upper_delay = jnp.take(delay_table, index_share + 1, axis=0)
    delay_share = lower_delay + fraction_share.astype(jnp.float32) * (1.0 / 65536.0) * (
        upper_delay - lower_delay
    )
    delays = gather_axes(delay_share, CHAN, (2, 0, 1, 3), 0).reshape(beam_count, local_stations)
    coeffs = prototype(TAPS, NFFT)
    history = passed_along(voltages[:, frames_dev - (TAPS - 1) :], CHAN, 1)
    filtered = polyphase(jnp.concatenate([history, voltages], axis=1), coeffs, frames_dev)
    dft_full = dft_table(NFFT)
    spectra = lax.dot_general(
        dft_full, filtered, (((0, 1), (2, 3)), ((), ())), preferred_element_type=jnp.float32
    ).astype(jnp.bfloat16)
    channel_ids = lax.axis_index(CHAN) * per_dev + jnp.arange(per_dev, dtype=jnp.int32)
    weights = steering(delays, station_subarray, channel_ids)
    spectra = spectra.reshape(2, groups_chan, per_dev, POL, frames_dev, local_stations)
    partial_value = lax.dot_general(
        weights,
        lax.all_to_all(spectra, CHAN, split_axis=1, concat_axis=1, tiled=True),
        (((3, 4), (0, 5)), ((0,), (2,))),
        preferred_element_type=jnp.float32,
    )
    summed = sent_and_summed(partial_value, "stn", 2).astype(jnp.bfloat16)
    ordered = jnp.transpose(summed, (1, 2, 4, 0, 3, 5))
    return ordered.reshape(2, summed.shape[2], POL, per_dev, groups_chan * frames_dev)


def solution(mesh):
    torus = Mesh(
        mesh.devices.reshape(8, 4, 2, 2, mesh.shape["stn"]),
        ("chan_0", "chan_1", "chan_2", "chan_3", "stn"),
    )
    placed = (P(None, CHAN, None, None, "stn"), P(), P(None, "stn"), P(None, "stn"), P("stn"))
    return jax.shard_map(
        shards,
        mesh=torus,
        in_specs=placed,
        out_specs=P(None, "stn", None, CHAN, None),
        check_vma=False,
    )
```

profile of v0, /device:TPU:1, one launch (start us, length us, event | category | flops | bytes accessed | tf_op | source)
XLA Modules:
  0.0 368.8 jit_solution(15485896743960134796)
XLA Ops:
  0.0 5.9 %slice.85 = bf16[2,11,2,256,256]{4,3,2,1,0:T(8,128)(2,1)} slice(bf16[2,12,2,256,256]{4,3,2,1,0:T(8,128)(2,1)} %param.7), slice={[0:2], [1:12], [0:2], [0:256], [0:256]} | slice | bytes 11534336 | tf_op jit(solution)/shard_map/slice | solution.py:116
  5.9 4.5 %collective-permute-start = (bf16[2,11,2,256,256]{4,3,2,1,0:T(8,128)(2,1)}, bf16[2,11,2,256,256]{4,3,2,1,0:T(8,128)(2,1)}, u32[]{:S(2)}, u32[]{:S(2)}) collective-permute-start(bf16[2,11,2,256,256]{4,3,2,1,0:T(8,128)(2,1)} %slice.85), channel_id=1, source_target_pairs={{0,2},{2,4},{4,6},{6,8},{8,10},{10,12},{12,14},{14,16},{16,18},{18... | collective-permute-start | bytes 17301512 | tf_op jit(solution)/shard_map/ppermute | solution.py:39
  10.4 0.7 multiply_reduce_fusion
  11.8 0.1 broadcast_multiply_fusion
  11.9 1.0 fusion.16
  12.9 1.1 negate_convert_fusion
  14.0 0.0 slice-start.1
  14.1 58.9 %collective-permute-done = bf16[2,11,2,256,256]{4,3,2,1,0:T(8,128)(2,1)} collective-permute-done((bf16[2,11,2,256,256]{4,3,2,1,0:T(8,128)(2,1)}, bf16[2,11,2,256,256]{4,3,2,1,0:T(8,128)(2,1)}, u32[]{:S(2)}, u32[]{:S(2)}) %collective-permute-start) | collective-permute-done | bytes 5767200 | tf_op jit(solution)/shard_map/ppermute | solution.py:39
  73.0 5.8 %constant_dynamic-update-slice_fusion.1 = bf16[2,23,2,256,256]{4,3,2,1,0:T(8,128)(2,1)} fusion(bf16[2,11,2,256,256]{4,3,2,1,0:T(8,128)(2,1)} %collective-permute-done), kind=kLoop, calls=%fused_computation.83 | loop fusion | bytes 11534336
  78.8 3.1 constant_dynamic-update-slice_fusion
  81.9 31.7 %bitcast_convert_fusion = bf16[2,256,2,12,256]{4,1,3,2,0:T(8,128)(2,1)} fusion(bf16[2,12,2,256,256]{4,3,2,1,0:T(8,128)(2,1)S(1)} %bitcast.60, f32[256]{0:T(256)S(1)} %get-tuple-element.15, bf16[2,23,2,256,256]{4,3,2,1,0:T(8,128)(2,1)} %constant_dynamic-update-slice_fusion, f32[256]{0:T(256)S(1)} %get-tuple-element.16, f32[256]{0:T(256)S(1)} %get-tuple-element.17, ...), kind=kOutput, calls=%fused_computation.2 | convolution fusion | flops 3338665984 | bytes 82325504 | tf_op jit(solution)/shard_map/dot_general | solution.py:119
  113.6 0.0 copy-start.2
  113.6 12.8 %copy.29 = bf16[2,256,2,12,256]{4,0,3,2,1:T(2,128)(2,1)} copy(bf16[2,256,2,12,256]{4,1,3,2,0:T(8,128)(2,1)} %bitcast_convert_fusion) | data formatting | bytes 12582912 | tf_op jit(solution)/shard_map/reshape | solution.py:124
  126.4 15.8 %all-to-all-start = ((bf16[2,128,2,2,12,256]{5,0,4,3,2,1:T(2,128)(2,1)}), bf16[2,128,2,2,12,256]{5,0,4,3,2,1:T(2,128)(2,1)}, u32[]{:S(2)}, u32[]{:S(2)}) async-start(bf16[2,128,2,2,12,256]{5,0,4,3,2,1:T(2,128)(2,1)} %bitcast.58), calls=%async_computation | async-start | bytes 12582912 | tf_op jit(solution)/shard_map/all_to_all | solution.py:127
  142.3 0.1 compare_select_fusion.2
  142.4 1.1 gather_fusion.1
  143.6 1.1 gather_fusion
  144.7 0.1 add_bitcast_fusion
  144.8 12.8 %all-gather.1 = f32[2,1,128]{2,1,0:T(1,128)S(1)} all-gather(f32[1,1,128]{2,1,0:T(1,128)S(1)} %add_bitcast_fusion), channel_id=2, replica_groups=mesh['chan_0'=8,'chan_1'=4,'chan_2'=2,'chan_3'=2,'stn'=2] {'chan_2'}, dimensions={0}, use_global_device_ids=true | all-gather | bytes 1536 | tf_op jit(solution)/shard_map/all_gather | solution.py:25
  157.6 128.6 %all-gather.2 = f32[8,2,128]{2,1,0:T(2,128)S(1)} all-gather(f32[1,2,128]{2,1,0:T(2,128)S(1)} %bitcast.75), channel_id=1, replica_groups=mesh['chan_0'=8,'chan_1'=4,'chan_2'=2,'chan_3'=2,'stn'=2] {'chan_0'}, dimensions={0}, use_global_device_ids=true | all-gather | bytes 9216 | tf_op jit(solution)/shard_map/all_gather | solution.py:25
  286.3 9.0 %all_gather.14 = f32[64,128]{1,0:T(8,128)S(1)} all-gather(f32[16,128]{1,0:T(8,128)S(1)} %bitcast.74), channel_id=1, replica_groups=mesh['chan_0'=8,'chan_1'=4,'chan_2'=2,'chan_3'=2,'stn'=2] {'chan_1'}, dimensions={0}, use_global_device_ids=true | all-gather | bytes 40960 | tf_op jit(solution)/shard_map/all_gather | solution.py:25
  295.3 7.9 %all_gather.15 = f32[128,128]{1,0:T(8,128)S(1)} all-gather(f32[64,128]{1,0:T(8,128)S(1)} %all_gather.14), channel_id=1, replica_groups=mesh['chan_0'=8,'chan_1'=4,'chan_2'=2,'chan_3'=2,'stn'=2] {'chan_3'}, dimensions={0}, use_global_device_ids=true | all-gather | bytes 98304 | tf_op jit(solution)/shard_map/all_gather | solution.py:25
  303.2 0.1 copy.15
  303.3 0.1 compare_select_fusion
  303.4 0.5 fusion.18
  303.9 0.5 fusion.57
  304.5 10.0 %fusion = f32[2,2,64,128,2,12,1]{3,2,6,5,4,1,0:T(8,128)S(1)} fusion(bf16[2,128,2,2,12,256,1]{5,0,4,3,2,1,6:T(2,128)(2,1)} %bitcast.19, bf16[2,1,64,2,256]{4,2,3,1,0:T(8,128)(2,1)S(1)} %get-tuple-element.11, bf16[2,1,64,2,256]{4,2,3,1,0:T(8,128)(2,1)S(1)} %get-tuple-element.10), kind=kOutput, calls=%fused_computation.4 | convolution fusion | flops 805830656 | bytes 9699328 | tf_op jit(solution)/shard_map/dot_general | solution.py:125
  314.5 0.4 copy.40
  314.9 40.8 %all_to_all.10 = f32[2,2,2,32,128,2,12]{4,3,6,5,2,1,0:T(8,128)S(1)} all-to-all(f32[2,2,2,32,128,2,12]{4,3,6,5,2,1,0:T(8,128)S(1)} %bitcast.61), channel_id=1, replica_groups=mesh['chan_0'=8,'chan_1'=4,'chan_2'=2,'chan_3'=2,'stn'=2] {'stn'}, dimensions={0} | all-to-all | bytes 6291456 | tf_op jit(solution)/shard_map/all_to_all | solution.py:50
  355.7 1.4 reduce_sum.19
  357.1 6.6 %copy.22 = bf16[2,32,2,2,128,12]{1,3,5,4,2,0:T(2,128)(2,1)S(1)} copy(bf16[2,32,2,2,128,12]{4,1,5,2,0,3:T(8,128)(2,1)} %bitcast.64) | data formatting | bytes 1572864 | tf_op jit(solution)/shard_map/convert_element_type | solution.py:131
  363.8 5.0 %copy.23 = bf16[2,32,2,2,1536]{4,3,2,1,0:T(2,128)(2,1)} copy(bf16[2,32,2,2,1536]{1,3,4,2,0:T(2,128)(2,1)S(1)} %bitcast.63) | data formatting | bytes 1572864 | tf_op jit(solution)/shard_map/reshape | solution.py:133
  (21 shorter events, 0.2 us)
Async XLA Ops:
  0.0 142.4 %copy-start = (f32[4096]{0:T(1024)S(1)}, f32[4096]{0:T(1024)}, u32[]{:S(2)}) copy-start(f32[4096]{0:T(1024)} %param.8) | copy-start | bytes 49156
  0.0 78.8 %slice-start = ((s8[6291456]{0:T(1024)(128)(4,1)}), s8[2097152]{0:T(1024)(128)(4,1)S(1)}, s32[]{:S(2)}) async-start(s8[6291456]{0:T(1024)(128)(4,1)} %bitcast.59), calls=%async_computation.2 | async-start | bytes 4194304
  5.9 67.1 %collective-permute-start = (bf16[2,11,2,256,256]{4,3,2,1,0:T(8,128)(2,1)}, bf16[2,11,2,256,256]{4,3,2,1,0:T(8,128)(2,1)}, u32[]{:S(2)}, u32[]{:S(2)}) collective-permute-start(bf16[2,11,2,256,256]{4,3,2,1,0:T(8,128)(2,1)} %slice.85), channel_id=1, source_target_pairs={{0,2},{2,4},{4,6},{6,8},{8,10},{10,12},{12,14},{14,16},{16,18},{18... | collective-permute-start | bytes 17301512 | tf_op jit(solution)/shard_map/ppermute | solution.py:39
  14.0 64.8 %slice-start.1 = ((s8[6291456]{0:T(1024)(128)(4,1)}), s8[4194304]{0:T(1024)(128)(4,1)S(1)}, s32[]{:S(2)}) async-start(s8[6291456]{0:T(1024)(128)(4,1)} %bitcast.59), calls=%async_computation.3 | async-start | bytes 8388608
  113.6 28.6 %copy-start.1 = (s32[64,256]{1,0:T(8,128)S(1)}, s32[64,256]{1,0:T(8,128)}, u32[]{:S(2)}) copy-start(s32[64,256]{1,0:T(8,128)} %param.10) | copy-start | bytes 196612
  113.6 28.7 %copy-start.2 = (s32[64,256]{1,0:T(8,128)S(1)}, s32[64,256]{1,0:T(8,128)}, u32[]{:S(2)}) copy-start(s32[64,256]{1,0:T(8,128)} %param.9) | copy-start | bytes 196612
  113.6 189.7 %copy-start.3 = (s32[256]{0:T(256)S(1)}, s32[256]{0:T(256)}, u32[]{:S(2)}) copy-start(s32[256]{0:T(256)} %param.11) | copy-start | bytes 3076
  126.4 178.0 %all-to-all-start = ((bf16[2,128,2,2,12,256]{5,0,4,3,2,1:T(2,128)(2,1)}), bf16[2,128,2,2,12,256]{5,0,4,3,2,1:T(2,128)(2,1)}, u32[]{:S(2)}, u32[]{:S(2)}) async-start(bf16[2,128,2,2,12,256]{5,0,4,3,2,1:T(2,128)(2,1)} %bitcast.58), calls=%async_computation | async-start | bytes 12582912 | tf_op jit(solution)/shard_map/all_to_all | solution.py:127
where the time goes:
time: 369 us
  blocking collectives  199 us (54%)
  waiting for transfers between devices  58.9 us (16%)
  local copies, waits for them, and re-layouts  42.1 us (11%)
  matrix products  41.7 us (11%)
  starting transfers between devices  20.3 us (6%)
  other arithmetic  5.62 us (2%)
    all_gather x4, blocking collectives, all_blocks(): parts = lax.all_gather(parts, axes[k], axis=0, tiled=True)  158 us
    ppermute x1, waiting for transfers between devices, passed_along(): lax.ppermute(value, axis, [(source, source + steps) for source in range(i...  58.9 us
    all_to_all x1, blocking collectives, sent_and_summed(): lax.all_to_all(parts, axis, split_axis=0, concat_axis=0, tiled=True)  40.8 us
    dot_general x1, matrix products, shards(): lax.dot_general(dft_full, filtered, (((0, 1), (2, 3)), ((), ())), preferr...  31.7 us
    all_to_all x1, starting transfers between devices, shards(): lax.all_to_all(spectra, CHAN, split_axis=1, concat_axis=1, tiled=True)  15.8 us
    reshape x1, local copies, waits for them, and re-layouts, shards(): spectra.reshape(2, groups_chan, per_dev, POL, frames_dev, local_stations)  12.8 us
    dot_general x1, matrix products, shards(): lax.dot_general(weights, lax.all_to_all(spectra, CHAN, split_axis=1, conc...  10 us
  transfers between devices with their start and end apart: 2, of which 1 were waited for; matrix products, arithmetic and copies ran while one was open for 2% of the time, Pallas kernels for 0%

commit v1 on v0

--- a/solution.py
+++ b/solution.py
@@ -13,6 +13,13 @@
 CHAN = ("chan_0", "chan_1", "chan_2", "chan_3")
 
 
+def exchange_gather(value, mesh_axis, d):
+    n_dev = lax.axis_size(mesh_axis)
+    parts = jnp.stack([value for _ in range(n_dev)])
+    parts = lax.all_to_all(parts, mesh_axis, split_axis=0, concat_axis=0)
+    return jnp.concatenate(parts, axis=d)
+
+
 def joined_along(parts, dim):
     shape = list(parts.shape[1:])
     shape[dim] *= parts.shape[0]
@@ -22,7 +29,7 @@
 def all_blocks(x, axes, turns):
     parts = x[None]
     for k in turns:
-        parts = lax.all_gather(parts, axes[k], axis=0, tiled=True)
+        parts = exchange_gather(parts, axes[k], 0)
     held = [lax.axis_size(axes[k]) for k in reversed(turns)]
     parts = parts.reshape(*held, *x.shape)
     turned = sorted(range(len(turns)), key=lambda place: turns[len(turns) - 1 - place])

time: 369 us -> 367 us (level)
  blocking collectives: 199 us -> 39 us
  waiting for transfers between devices: 58.9 us -> 200 us
  starting transfers between devices: 20.3 us -> 30 us
    all_gather x4 -> x0, blocking collectives: 158 us -> none  [all_blocks(): parts = lax.all_gather(parts, axes[k], axis=0, tiled=True)]
    all_to_all x1, waiting for transfers between devices: 0.01 us -> 137 us  [shards(): lax.all_to_all(spectra, CHAN, split_axis=1, concat_axis=1, tiled=True)]
    all_to_all x0 -> x4, waiting for transfers between devices: none -> 63.6 us  [exchange_gather(): parts = lax.all_to_all(parts, mesh_axis, split_axis=0, concat_axis=0)]
    ppermute x1, waiting for transfers between devices: 58.9 us -> 0.01 us  [passed_along(): lax.ppermute(value, axis, [(source, source + steps) for source in range(i...]
    all_to_all x0 -> x4, starting transfers between devices: none -> 18.7 us  [exchange_gather(): parts = lax.all_to_all(parts, mesh_axis, split_axis=0, concat_axis=0)]
    all_to_all x1, starting transfers between devices: 15.8 us -> 6.69 us  [shards(): lax.all_to_all(spectra, CHAN, split_axis=1, concat_axis=1, tiled=True)]
    unnamed x16 -> x12, local copies, waits for them, and re-layouts: 5.88 us -> 7.69 us
  transfers between devices with their start and end apart: 2 -> 6, of which waited for: 1 -> 4; matrix products, arithmetic and copies ran while one was open for 2% -> 18% of each run, Pallas kernels for 0% -> 0%
where the time goes in v1:
time: 367 us; the launch traced here: 364 us
  waiting for transfers between devices  200 us (54%)
  local copies, waits for them, and re-layouts  45 us (12%)
  matrix products  41.7 us (11%)
  blocking collectives  39 us (11%)
  starting transfers between devices  30 us (8%)
  other arithmetic  6.9 us (2%)
    all_to_all x1, waiting for transfers between devices, shards(): lax.all_to_all(spectra, CHAN, split_axis=1, concat_axis=1, tiled=True)  137 us
    all_to_all x4, waiting for transfers between devices, exchange_gather(): parts = lax.all_to_all(parts, mesh_axis, split_axis=0, concat_axis=0)  63.6 us
    all_to_all x1, blocking collectives, sent_and_summed(): lax.all_to_all(parts, axis, split_axis=0, concat_axis=0, tiled=True)  39 us
    dot_general x1, matrix products, shards(): lax.dot_general(dft_full, filtered, (((0, 1), (2, 3)), ((), ())), preferr...  31.7 us
    all_to_all x4, starting transfers between devices, exchange_gather(): parts = lax.all_to_all(parts, mesh_axis, split_axis=0, concat_axis=0)  18.7 us
    reshape x1, local copies, waits for them, and re-layouts, shards(): spectra.reshape(2, groups_chan, per_dev, POL, frames_dev, local_stations)  12.8 us
    dot_general x1, matrix products, shards(): lax.dot_general(weights, lax.all_to_all(spectra, CHAN, split_axis=1, conc...  10 us
    unnamed x12, local copies, waits for them, and re-layouts  7.69 us
  transfers between devices with their start and end apart: 6, of which 4 were waited for; matrix products, arithmetic and copies ran while one was open for 18% of the time, Pallas kernels for 0%

profile of v1, /device:TPU:1, one launch (start us, length us, event | category | flops | bytes accessed | tf_op | source)
XLA Modules:
  0.0 363.8 jit_solution(14613273201415638754)
XLA Ops:
  0.0 5.8 %slice.85 = bf16[2,11,2,256,256]{4,3,2,1,0:T(8,128)(2,1)} slice(bf16[2,12,2,256,256]{4,3,2,1,0:T(8,128)(2,1)} %param.7), slice={[0:2], [1:12], [0:2], [0:256], [0:256]} | slice | bytes 11534336 | tf_op jit(solution)/shard_map/slice | solution.py:123
  5.8 4.6 %collective-permute-start = (bf16[2,11,2,256,256]{4,3,2,1,0:T(8,128)(2,1)}, bf16[2,11,2,256,256]{4,3,2,1,0:T(8,128)(2,1)}, u32[]{:S(2)}, u32[]{:S(2)}) collective-permute-start(bf16[2,11,2,256,256]{4,3,2,1,0:T(8,128)(2,1)} %slice.85), channel_id=1, source_target_pairs={{0,2},{2,4},{4,6},{6,8},{8,10},{10,12},{12,14},{14,16},{16,18},{18... | collective-permute-start | bytes 17301512 | tf_op jit(solution)/shard_map/ppermute | solution.py:46
  10.4 0.9 copy.37
  11.3 0.9 copy.36
  12.3 1.1 gather_fusion.1
  13.4 1.1 gather_fusion
  14.7 0.6 pad_maximum_fusion.1
  15.3 3.2 all-to-all-start
  18.5 0.8 multiply_reduce_fusion
  20.1 1.1 negate_convert_fusion
  21.2 53.8 %all-to-all-done = f32[2,1,128]{2,1,0:T(1,128)S(1)} async-done(((f32[2,1,128]{2,1,0:T(1,128)}), f32[2,1,128]{2,1,0:T(1,128)S(1)}, u32[]{:S(2)}, u32[]{:S(2)}) %all-to-all-start) | async-done | bytes 1056 | tf_op jit(solution)/shard_map/all_to_all | solution.py:19
  75.0 0.6 stack.56
  75.6 8.3 %all-to-all-start.1 = ((f32[8,2,128]{2,1,0:T(2,128)}), f32[8,2,128]{2,1,0:T(2,128)S(1)}, u32[]{:S(2)}, u32[]{:S(2)}) async-start(f32[8,2,128]{2,1,0:T(2,128)} %stack.56), calls=%async_computation.1 | async-start | bytes 16384 | tf_op jit(solution)/shard_map/all_to_all | solution.py:19
  83.9 1.0 fusion.16
  84.8 5.6 %all-to-all-done.1 = f32[8,2,128]{2,1,0:T(2,128)S(1)} async-done(((f32[8,2,128]{2,1,0:T(2,128)}), f32[8,2,128]{2,1,0:T(2,128)S(1)}, u32[]{:S(2)}, u32[]{:S(2)}) %all-to-all-start.1) | async-done | bytes 8224 | tf_op jit(solution)/shard_map/all_to_all | solution.py:19
  90.4 0.6 stack.57
  91.1 3.9 %all-to-all-start.2 = ((f32[4,16,128]{2,1,0:T(8,128)}), f32[4,16,128]{2,1,0:T(8,128)S(1)}, u32[]{:S(2)}, u32[]{:S(2)}) async-start(f32[4,16,128]{2,1,0:T(8,128)} %stack.57), calls=%async_computation.2 | async-start | bytes 65536 | tf_op jit(solution)/shard_map/all_to_all | solution.py:19
  95.0 4.3 %all-to-all-done.2 = f32[4,16,128]{2,1,0:T(8,128)S(1)} async-done(((f32[4,16,128]{2,1,0:T(8,128)}), f32[4,16,128]{2,1,0:T(8,128)S(1)}, u32[]{:S(2)}, u32[]{:S(2)}) %all-to-all-start.2) | async-done | bytes 32800 | tf_op jit(solution)/shard_map/all_to_all | solution.py:19
  99.2 0.6 pad_maximum_fusion
  99.9 3.3 all-to-all-start.3
  103.2 5.9 %constant_dynamic-update-slice_fusion.1 = bf16[2,23,2,256,256]{4,3,2,1,0:T(8,128)(2,1)} fusion(bf16[2,11,2,256,256]{4,3,2,1,0:T(8,128)(2,1)} %collective-permute-done), kind=kLoop, calls=%fused_computation.84 | loop fusion | bytes 11534336
  109.1 3.1 constant_dynamic-update-slice_fusion
  112.2 31.7 %bitcast_convert_fusion = bf16[2,256,2,12,256]{4,1,3,2,0:T(8,128)(2,1)} fusion(bf16[2,12,2,256,256]{4,3,2,1,0:T(8,128)(2,1)S(1)} %bitcast.62, f32[256]{0:T(256)S(1)} %get-tuple-element.15, bf16[2,23,2,256,256]{4,3,2,1,0:T(8,128)(2,1)} %constant_dynamic-update-slice_fusion, f32[256]{0:T(256)S(1)} %get-tuple-element.16, f32[256]{0:T(256)S(1)} %get-tuple-element.17, ...), kind=kOutput, calls=%fused_computation.2 | convolution fusion | flops 3338665984 | bytes 82325504 | tf_op jit(solution)/shard_map/dot_general | solution.py:126
  143.9 12.8 %copy.32 = bf16[2,256,2,12,256]{4,0,3,2,1:T(2,128)(2,1)} copy(bf16[2,256,2,12,256]{4,1,3,2,0:T(8,128)(2,1)} %bitcast_convert_fusion) | data formatting | bytes 12582912 | tf_op jit(solution)/shard_map/reshape | solution.py:131
  156.7 6.7 %all-to-all-start.4 = ((bf16[2,128,2,2,12,256]{5,0,4,3,2,1:T(2,128)(2,1)}), bf16[2,128,2,2,12,256]{5,0,4,3,2,1:T(2,128)(2,1)}, u32[]{:S(2)}, u32[]{:S(2)}) async-start(bf16[2,128,2,2,12,256]{5,0,4,3,2,1:T(2,128)(2,1)} %bitcast.60), calls=%async_computation.4 | async-start | bytes 12582912 | tf_op jit(solution)/shard_map/all_to_all | solution.py:134
  164.1 0.5 fusion.57
  164.6 136.6 %all-to-all-done.4 = bf16[2,128,2,2,12,256]{5,0,4,3,2,1:T(2,128)(2,1)} async-done(((bf16[2,128,2,2,12,256]{5,0,4,3,2,1:T(2,128)(2,1)}), bf16[2,128,2,2,12,256]{5,0,4,3,2,1:T(2,128)(2,1)}, u32[]{:S(2)}, u32[]{:S(2)}) %all-to-all-start.4) | async-done | bytes 6291488 | tf_op jit(solution)/shard_map/all_to_all | solution.py:134
  301.3 10.0 %fusion = f32[2,2,64,128,2,12,1]{3,2,6,5,4,1,0:T(8,128)S(1)} fusion(bf16[2,128,2,2,12,256,1]{5,0,4,3,2,1,6:T(2,128)(2,1)} %bitcast.20, bf16[2,1,64,2,256]{4,2,3,1,0:T(8,128)(2,1)S(1)} %get-tuple-element.11, bf16[2,1,64,2,256]{4,2,3,1,0:T(8,128)(2,1)S(1)} %get-tuple-element.10), kind=kOutput, calls=%fused_computation.4 | convolution fusion | flops 805830656 | bytes 9699328 | tf_op jit(solution)/shard_map/dot_general | solution.py:132
  311.7 39.0 %all_to_all.30 = f32[2,2,2,32,128,2,12]{4,3,6,5,2,1,0:T(8,128)S(1)} all-to-all(f32[2,2,2,32,128,2,12]{4,3,6,5,2,1,0:T(8,128)S(1)} %bitcast.63), channel_id=1, replica_groups=mesh['chan_0'=8,'chan_1'=4,'chan_2'=2,'chan_3'=2,'stn'=2] {'stn'}, dimensions={0} | all-to-all | bytes 6291456 | tf_op jit(solution)/shard_map/all_to_all | solution.py:57
  350.7 1.4 reduce_sum.19
  352.1 6.6 %copy.25 = bf16[2,32,2,2,128,12]{1,3,5,4,2,0:T(2,128)(2,1)S(1)} copy(bf16[2,32,2,2,128,12]{4,1,5,2,0,3:T(8,128)(2,1)} %bitcast.66) | data formatting | bytes 1572864 | tf_op jit(solution)/shard_map/convert_element_type | solution.py:138
  358.8 5.0 %copy.26 = bf16[2,32,2,2,1536]{4,3,2,1,0:T(2,128)(2,1)} copy(bf16[2,32,2,2,1536]{1,3,4,2,0:T(2,128)(2,1)S(1)} %bitcast.65) | data formatting | bytes 1572864 | tf_op jit(solution)/shard_map/reshape | solution.py:140
  (25 shorter events, 1.4 us)
Async XLA Ops:
  0.0 12.3 %copy-start = (f32[4096]{0:T(1024)S(1)}, f32[4096]{0:T(1024)}, u32[]{:S(2)}) copy-start(f32[4096]{0:T(1024)} %param.8) | copy-start | bytes 49156
  5.8 103.3 %slice-start = ((s8[6291456]{0:T(1024)(128)(4,1)}), s8[2097152]{0:T(1024)(128)(4,1)S(1)}, s32[]{:S(2)}) async-start(s8[6291456]{0:T(1024)(128)(4,1)} %bitcast.61), calls=%async_computation.6 | async-start | bytes 4194304
  5.8 97.4 %collective-permute-start = (bf16[2,11,2,256,256]{4,3,2,1,0:T(8,128)(2,1)}, bf16[2,11,2,256,256]{4,3,2,1,0:T(8,128)(2,1)}, u32[]{:S(2)}, u32[]{:S(2)}) collective-permute-start(bf16[2,11,2,256,256]{4,3,2,1,0:T(8,128)(2,1)} %slice.85), channel_id=1, source_target_pairs={{0,2},{2,4},{4,6},{6,8},{8,10},{10,12},{12,14},{14,16},{16,18},{18... | collective-permute-start | bytes 17301512 | tf_op jit(solution)/shard_map/ppermute | solution.py:46
  15.3 59.7 %all-to-all-start = ((f32[2,1,128]{2,1,0:T(1,128)}), f32[2,1,128]{2,1,0:T(1,128)S(1)}, u32[]{:S(2)}, u32[]{:S(2)}) async-start(f32[2,1,128]{2,1,0:T(1,128)} %pad_maximum_fusion.1), calls=%async_computation | async-start | bytes 2048 | tf_op jit(solution)/shard_map/all_to_all | solution.py:19
  75.6 14.9 %all-to-all-start.1 = ((f32[8,2,128]{2,1,0:T(2,128)}), f32[8,2,128]{2,1,0:T(2,128)S(1)}, u32[]{:S(2)}, u32[]{:S(2)}) async-start(f32[8,2,128]{2,1,0:T(2,128)} %stack.56), calls=%async_computation.1 | async-start | bytes 16384 | tf_op jit(solution)/shard_map/all_to_all | solution.py:19
  91.1 8.2 %all-to-all-start.2 = ((f32[4,16,128]{2,1,0:T(8,128)}), f32[4,16,128]{2,1,0:T(8,128)S(1)}, u32[]{:S(2)}, u32[]{:S(2)}) async-start(f32[4,16,128]{2,1,0:T(8,128)} %stack.57), calls=%async_computation.2 | async-start | bytes 65536 | tf_op jit(solution)/shard_map/all_to_all | solution.py:19
  99.9 56.8 %all-to-all-start.3 = ((f32[2,64,128]{2,1,0:T(8,128)}), f32[2,64,128]{2,1,0:T(8,128)S(1)}, u32[]{:S(2)}, u32[]{:S(2)}) async-start(f32[2,64,128]{2,1,0:T(8,128)} %pad_maximum_fusion), calls=%async_computation.3 | async-start | bytes 131072 | tf_op jit(solution)/shard_map/all_to_all | solution.py:19
  103.2 5.9 %slice-start.1 = ((s8[6291456]{0:T(1024)(128)(4,1)}), s8[4194304]{0:T(1024)(128)(4,1)S(1)}, s32[]{:S(2)}) async-start(s8[6291456]{0:T(1024)(128)(4,1)} %bitcast.61), calls=%async_computation.7 | async-start | bytes 8388608
  143.9 19.5 %copy-start.1 = (s32[256]{0:T(256)S(1)}, s32[256]{0:T(256)}, u32[]{:S(2)}) copy-start(s32[256]{0:T(256)} %param.11) | copy-start | bytes 3076
  156.7 144.6 %all-to-all-start.4 = ((bf16[2,128,2,2,12,256]{5,0,4,3,2,1:T(2,128)(2,1)}), bf16[2,128,2,2,12,256]{5,0,4,3,2,1:T(2,128)(2,1)}, u32[]{:S(2)}, u32[]{:S(2)}) async-start(bf16[2,128,2,2,12,256]{5,0,4,3,2,1:T(2,128)(2,1)} %bitcast.60), calls=%async_computation.4 | async-start | bytes 12582912 | tf_op jit(solution)/shard_map/all_to_all | solution.py:134
